TPU v7x, 32 devices: a whole 2x2x4 slice. The times are simulated.
32 devices in a mesh: dp: 4 (over y, core), tower: 8 (over z, x).
Axes of the slice: x: 2, y: 2, z: 4, core: 2. Of those that a mesh axis runs over, the one named last changes fastest.
Arguments:
- attn_out: bfloat16 [4096, 4096], P(('dp', 'tower')), may hold values from -0.375 to 0.375
- out_cot: bfloat16 [4096, 4096], P(('dp', 'tower')), may hold values from -6 to 6
- modality: int32 [4096], P(('dp', 'tower')), may hold values from 0 to 2, as said below
- group_modality: int32 [8], replicated, may hold values from 0 to 2, as said below
- o_weight: bfloat16 [32768, 4096], P('tower'), as said below
Outputs:
- attn_grad: bfloat16 [4096, 4096], P(('dp', 'tower'))
- weight_grad: bfloat16 [32768, 4096], P('tower', 'dp')
Inputs may be any that keep to these rules, and one draw needn't show every extreme that they name: `group_modality`: every modality is served by at least one group. In each block of 128 tokens (one device's tokens), a modality served by k groups appears at most k * 24 times; in every block the modality served by the fewest groups (the lowest such id on a tie) appears exactly that often. `o_weight`: groups that serve the same modality hold equal rows.
All inputs are finite; a program needn't handle non-finite values.
Results may differ from a plain program's by a relative error of at most 0.014.
Values may be sent and summed in bfloat16 or wider, within the bound.
No kernel may reach another device: no remote copies, remote signals or barrier semaphores. Data moves between devices by JAX's collectives and lax.ppermute only.
A program may use at most 128 MiB of HBM per device.

v0:
```python
import jax
import jax.numpy as jnp
from jax import lax
from jax.sharding import PartitionSpec as P

NGROUP = 8
CAP = 24


def routing(modal_rows, tower_idx, group_modality):
    modal_ids = jnp.arange(3, dtype=jnp.int32)
    member = (modal_rows[:, None] == modal_ids[None, :]).astype(jnp.int32)
    before = jnp.cumsum(member, axis=0) - member
    order_in = jnp.sum(before * member, axis=1)
    group_of = (group_modality[:, None] == modal_ids[None, :]).astype(jnp.int32)
    per_kind = jnp.sum(group_of, axis=0)
    group_rank = jnp.sum((jnp.cumsum(group_of, axis=0) - group_of) * group_of, axis=1)
    how_many = jnp.sum(member * per_kind[None, :], axis=1)
    target = (order_in + tower_idx) % how_many
    chosen = (group_modality[None, :] == modal_rows[:, None]) & (
        group_rank[None, :] == target[:, None]
    )
    group_ids = jnp.arange(group_modality.shape[0], dtype=jnp.int32)
    routed = jnp.sum(chosen.astype(jnp.int32) * group_ids[None, :], axis=1)
    slot_idx = order_in // how_many
    return (routed, slot_idx)


def per_device(attn_out, out_cot, modality, group_modality, o_weight):
    tower_idx = lax.axis_index("tower")
    tower_count = lax.axis_size("tower")
    group_size = tower_count // NGROUP
    piece_rows = o_weight.shape[0]
    model_width = attn_out.shape[1]
    tok_count = attn_out.shape[0]
    first_col = tower_idx % group_size * piece_rows
    routed, slot_idx = routing(modality, tower_idx, group_modality)
    group_ids = jnp.arange(NGROUP, dtype=jnp.int32)
    slot_ids = jnp.arange(CAP, dtype=jnp.int32)
    dispatch = (
        (routed[None, None, :] == group_ids[:, None, None])
        & (slot_idx[None, None, :] == slot_ids[None, :, None])
    ).astype(jnp.bfloat16)
    cot_group = jnp.einsum(
        "gct,te->gce", dispatch, out_cot, preferred_element_type=jnp.float32
    ).astype(jnp.bfloat16)
    cot_send = jnp.broadcast_to(cot_group[:, None], (NGROUP, group_size, CAP, model_width)).reshape(
        tower_count, CAP, model_width
    )
    attn_group = jnp.einsum(
        "gct,te->gce", dispatch, attn_out, preferred_element_type=jnp.float32
    ).astype(jnp.bfloat16)
    attn_send = jnp.broadcast_to(
        attn_group[:, None], (NGROUP, group_size, CAP, model_width)
    ).reshape(tower_count, CAP, model_width)
    attn_got = lax.all_to_all(attn_send, "tower", split_axis=0, concat_axis=0, tiled=True)
    cot_got = lax.all_to_all(cot_send, "tower", split_axis=0, concat_axis=0, tiled=True)
    attn_use = lax.dynamic_slice_in_dim(attn_got, first_col, piece_rows, 2)
    grad_piece = lax.dot_general(
        cot_got, o_weight, (((2,), (1,)), ((), ())), preferred_element_type=jnp.float32
    ).astype(jnp.bfloat16)
    returned = lax.all_to_all(grad_piece, "tower", split_axis=0, concat_axis=0, tiled=True)
    returned, attn_use, cot_got = (returned, attn_use, cot_got)
    returned_groups = returned.reshape(NGROUP, group_size, CAP, piece_rows)
    attn_grad = jnp.einsum(
        "gct,gpce->tpe", dispatch, returned_groups, preferred_element_type=jnp.float32
    )
    attn_grad = attn_grad.reshape(tok_count, model_width).astype(jnp.bfloat16)
    attn_rows = attn_use.reshape(tower_count * CAP, piece_rows)
    cot_rows = cot_got.reshape(tower_count * CAP, model_width)
    summed = lax.psum_scatter(
        lax.dot_general(
            cot_rows, attn_rows, (((0,), (0,)), ((), ())), preferred_element_type=jnp.float32
        ).astype(jnp.bfloat16),
        "dp",
        scatter_dimension=0,
        tiled=True,
    ).astype(jnp.float32)
    weight_grad = summed.T.astype(jnp.bfloat16)
    return (attn_grad, weight_grad)


def solution(mesh):
    return jax.shard_map(
        per_device,
        mesh=mesh,
        in_specs=(
            P(("dp", "tower"), None),
            P(("dp", "tower"), None),
            P(("dp", "tower")),
            P(),
            P("tower", None),
        ),
        out_specs=(P(("dp", "tower"), None), P("tower", "dp")),
        check_vma=False,
    )
```

profile of v0, /device:TPU:0, one launch (start us, length us, event | category | flops | bytes accessed | tf_op | source)
XLA Modules:
  0.0 365.1 jit_solution(394427249907986216)
XLA Ops:
  7.2 0.0 copy-start
  7.2 0.7 fusion.18
  7.9 0.2 reduce_window_sum.22
  8.1 0.8 select_reduce_fusion.3
  8.9 0.7 fusion.11
  9.6 0.2 reduce_window_sum.23
  9.8 0.8 select_reduce_fusion
  10.7 0.1 and_select_fusion.1
  10.8 0.8 select_reduce_fusion.2
  11.6 0.0 copy-done
  11.6 1.7 convolution_convert_fusion
  13.3 0.0 copy-start.4
  13.3 7.4 %all-to-all-start.2 = ((bf16[8,24,4096]{2,1,0:T(8,128)(2,1)}), bf16[8,24,4096]{2,1,0:T(8,128)(2,1)}, u32[]{:S(2)}, u32[]{:S(2)}) async-start(bf16[8,24,4096]{2,1,0:T(8,128)(2,1)} %convolution_convert_fusion), calls=%async_computation.2 | async-start | bytes 3145728 | tf_op jit(solution)/shard_map/all_to_all | solution.py:56
  20.7 0.0 reduce-scatter.4.cloned.1.call-start
  20.7 0.0 copy-done.4
  20.8 0.6 convolution_convert_fusion.1
  21.3 36.5 %all-to-all-done.2 = bf16[8,24,4096]{2,1,0:T(8,128)(2,1)} async-done(((bf16[8,24,4096]{2,1,0:T(8,128)(2,1)}), bf16[8,24,4096]{2,1,0:T(8,128)(2,1)}, u32[]{:S(2)}, u32[]{:S(2)}) %all-to-all-start.2) | async-done | bytes 1572896 | tf_op jit(solution)/shard_map/all_to_all | solution.py:56
  57.8 40.6 %all_to_all.15 = bf16[8,24,4096]{2,1,0:T(8,128)(2,1)S(1)} all-to-all(bf16[8,24,4096]{2,1,0:T(8,128)(2,1)S(1)} %convolution_convert_fusion.1), channel_id=1, replica_groups=mesh['dp'=4,'tower'=8] {'tower'}, dimensions={0} | all-to-all | bytes 3145728 | tf_op jit(solution)/shard_map/all_to_all | solution.py:57
  98.4 0.0 copy-start.2
  98.4 1.1 copy-done.2
  99.5 15.1 %bitcast_convert_fusion = bf16[4096,4096]{1,0:T(8,128)(2,1)} fusion(bf16[8,24,4096]{2,1,0:T(8,128)(2,1)S(1)} %all_to_all.15, bf16[8,24,4096]{2,1,0:T(8,128)(2,1)} %all-to-all-done.2), kind=kOutput, calls=%fused_computation | convolution fusion | flops 6459228160 | bytes 36700160 | tf_op jit(solution)/shard_map/dot_general | solution.py:72
  114.6 0.0 copy-start.3
  114.6 0.0 reduce-scatter.4.cloned.1.call-update
  114.7 1.4 copy-done.3
  116.1 21.2 %fusion.2 = bf16[8,24,4096]{2,1,0:T(8,128)(2,1)S(1)} fusion(bf16[8,24,4096]{2,1,0:T(8,128)(2,1)S(1)} %copy-done.3, bf16[4096,4096]{1,0:T(8,128)(2,1)} %param.9), kind=kOutput, calls=%fused_computation.3 | convolution fusion | flops 6443237376 | bytes 36700160 | tf_op jit(solution)/shard_map/dot_general | solution.py:59
  137.2 38.6 %all_to_all.16 = bf16[8,24,4096]{2,1,0:T(8,128)(2,1)S(1)} all-to-all(bf16[8,24,4096]{2,1,0:T(8,128)(2,1)S(1)} %fusion.2), channel_id=1, replica_groups=mesh['dp'=4,'tower'=8] {'tower'}, dimensions={0} | all-to-all | bytes 3145728 | tf_op jit(solution)/shard_map/all_to_all | solution.py:62
  175.9 1.5 fusion.5
  177.3 168.9 %reduce-scatter.4.cloned.1.call-done = bf16[1024,4096]{1,0:T(8,128)(2,1)} async-done(((bf16[4096,4096]{1,0:T(8,128)(2,1)}), bf16[1024,4096]{1,0:T(8,128)(2,1)}) %reduce-scatter.4.cloned.1.call-update) | async-done | bytes 8388624
  346.2 0.0 copy-start.1
  346.2 12.0 %copy.9 = bf16[4096,1024]{1,0:T(8,128)(2,1)} copy(bf16[4096,1024]{0,1:T(8,128)(2,1)} %bitcast.23) | data formatting | bytes 16777216
  358.2 0.0 copy-done.1
  (2 shorter events, 0.0 us)
Async XLA Ops:
  7.2 4.4 %copy-start = (bf16[128,4096]{1,0:T(8,128)(2,1)S(1)}, bf16[128,4096]{1,0:T(8,128)(2,1)}, u32[]{:S(2)}) copy-start(bf16[128,4096]{1,0:T(8,128)(2,1)} %param.5) | copy-start | bytes 3145732
  13.3 7.5 %copy-start.4 = (bf16[128,4096]{1,0:T(8,128)(2,1)S(1)}, bf16[128,4096]{1,0:T(8,128)(2,1)}, u32[]{:S(2)}) copy-start(bf16[128,4096]{1,0:T(8,128)(2,1)} %param.6) | copy-start | bytes 3145732
  13.3 44.5 %all-to-all-start.2 = ((bf16[8,24,4096]{2,1,0:T(8,128)(2,1)}), bf16[8,24,4096]{2,1,0:T(8,128)(2,1)}, u32[]{:S(2)}, u32[]{:S(2)}) async-start(bf16[8,24,4096]{2,1,0:T(8,128)(2,1)} %convolution_convert_fusion), calls=%async_computation.2 | async-start | bytes 3145728 | tf_op jit(solution)/shard_map/all_to_all | solution.py:56
  20.7 325.5 %reduce-scatter.4.cloned.1.call-start = ((), (), s32[]{:S(2)}) async-start(), calls=%async_computation.4 | async-start | bytes 41943040
  98.4 1.1 copy-start.2
  114.6 1.4 copy-start.3
  346.2 12.0 %copy-start.1 = (bf16[128,4096]{1,0:T(8,128)(2,1)S(1)}, bf16[128,4096]{1,0:T(8,128)(2,1)}, u32[]{:S(2)}) copy-start(bf16[128,4096]{1,0:T(8,128)(2,1)} %param.5) | copy-start | bytes 3145732
Sparse Core Ops, SparseCore 0:
  114.8 231.3 reduce-scatter.3
where the time goes:
time: 366 us; the launch traced here: 365 us
  waiting for transfers between devices  205 us (56%)
  blocking collectives  79.2 us (22%)
  matrix products  40 us (11%)
  local copies, waits for them, and re-layouts  14.6 us (4%)
  between operations  14.1 us (4%)
  starting transfers between devices  7.45 us (2%)
  other arithmetic  4.36 us (1%)
    unnamed x2, waiting for transfers between devices  169 us
    all_to_all x1, blocking collectives, per_device(): lax.all_to_all(cot_send, 'tower', split_axis=0, concat_axis=0, tiled=True)  40.6 us
    all_to_all x1, blocking collectives, per_device(): lax.all_to_all(grad_piece, 'tower', split_axis=0, concat_axis=0, tiled=True)  38.6 us
    all_to_all x1, waiting for transfers between devices, per_device(): lax.all_to_all(attn_send, 'tower', split_axis=0, concat_axis=0, tiled=True)  36.5 us
    dot_general x1, matrix products, per_device(): lax.dot_general(cot_got, o_weight, (((2,), (1,)), ((), ())), preferred_el...  21.2 us
    dot_general x1, matrix products, per_device(): lax.dot_general(cot_rows, attn_rows, (((0,), (0,)), ((), ())), preferred_...  15.1 us
    unnamed x11, local copies, waits for them, and re-layouts  14.6 us
    all_to_all x1, starting transfers between devices, per_device(): lax.all_to_all(attn_send, 'tower', split_axis=0, concat_axis=0, tiled=True)  7.41 us
  transfers between devices with their start and end apart: 2, of which 2 were waited for; matrix products, arithmetic and copies ran while one was open for 6% of the time, Pallas kernels for 0%

commit v1 on v0

v1 whole, which is shorter than its diff:
```python
import jax
import jax.numpy as jnp
from jax import lax
from jax.experimental import pallas as pl
from jax.experimental.pallas import tpu as pltpu
from jax.sharding import PartitionSpec as P

NGROUP = 8
CAP = 24
BF16 = jnp.bfloat16
F32 = jnp.float32


def routing(modal_rows, tower_idx, group_modality):
    modal_ids = jnp.arange(3, dtype=jnp.int32)
    member = (modal_rows[:, None] == modal_ids[None, :]).astype(jnp.int32)
    before = jnp.cumsum(member, axis=0) - member
    order_in = jnp.sum(before * member, axis=1)
    group_of = (group_modality[:, None] == modal_ids[None, :]).astype(jnp.int32)
    per_kind = jnp.sum(group_of, axis=0)
    group_rank = jnp.sum((jnp.cumsum(group_of, axis=0) - group_of) * group_of, axis=1)
    how_many = jnp.sum(member * per_kind[None, :], axis=1)
    target = (order_in + tower_idx) % how_many
    chosen = (group_modality[None, :] == modal_rows[:, None]) & (
        group_rank[None, :] == target[:, None]
    )
    group_ids = jnp.arange(group_modality.shape[0], dtype=jnp.int32)
    routed = jnp.sum(chosen.astype(jnp.int32) * group_ids[None, :], axis=1)
    slot_idx = order_in // how_many
    return (routed, slot_idx)


def weight_grad_kernel(count, *refs):
    attn_refs, cot_refs, out_ref = refs[:count], refs[count : 2 * count], refs[2 * count]
    total = None
    for attn_ref, cot_ref in zip(attn_refs, cot_refs):
        term = lax.dot_general(
            attn_ref[...], cot_ref[...], (((0,), (0,)), ((), ())), preferred_element_type=F32
        )
        total = term if total is None else total + term
    out_ref[...] = total.astype(out_ref.dtype)


def weight_grad_of(attn_parts, cot_parts):
    count = len(attn_parts)
    rows, features = attn_parts[0].shape
    columns = cot_parts[0].shape[1]
    block = min(512, features)
    return pl.pallas_call(
        lambda *refs: weight_grad_kernel(count, *refs),
        grid=(features // block,),
        in_specs=[pl.BlockSpec((rows, block), lambda i: (0, i))] * count
        + [pl.BlockSpec((rows, columns), lambda i: (0, 0))] * count,
        out_specs=pl.BlockSpec((block, columns), lambda i: (i, 0)),
        out_shape=jax.ShapeDtypeStruct((features, columns), BF16),
        cost_estimate=pl.CostEstimate(
            flops=2 * count * rows * features * columns,
            bytes_accessed=2 * (count * rows * (features + columns) + features * columns),
            transcendentals=0,
        ),
    )(*attn_parts, *cot_parts)


def per_device(attn_out, out_cot, modality, group_modality, o_weight):
    tower_idx = lax.axis_index("tower")
    tower_count = lax.axis_size("tower")
    dp_idx = lax.axis_index("dp")
    dp_count = lax.axis_size("dp")
    group_size = tower_count // NGROUP
    piece_rows = o_weight.shape[0]
    tok_count, model_width = attn_out.shape
    slot_rows = tower_count * CAP
    piece_cols = model_width // dp_count
    routed, slot_idx = routing(modality, tower_idx, group_modality)
    place = routed * CAP + slot_idx
    slots = jnp.arange(NGROUP * CAP, dtype=jnp.int32)
    dispatch = (place[None, :] == slots[:, None]).astype(BF16)

    cot_group = jnp.dot(dispatch, out_cot, preferred_element_type=F32).astype(BF16)
    attn_group = jnp.dot(dispatch, attn_out, preferred_element_type=F32).astype(BF16)
    cot_send = jnp.broadcast_to(
        cot_group.reshape(NGROUP, 1, CAP, model_width), (NGROUP, group_size, CAP, model_width)
    ).reshape(tower_count, CAP, model_width)
    attn_send = (
        attn_group.reshape(NGROUP, CAP, group_size, piece_rows)
        .transpose(0, 2, 1, 3)
        .reshape(tower_count, CAP, piece_rows)
    )
    cot_got = lax.all_to_all(cot_send, "tower", split_axis=0, concat_axis=0, tiled=True)
    attn_got = lax.all_to_all(attn_send, "tower", split_axis=0, concat_axis=0, tiled=True)
    cot_rows = cot_got.reshape(slot_rows, model_width)
    attn_rows = attn_got.reshape(slot_rows, piece_rows)

    grad_piece = lax.dot_general(
        cot_rows, o_weight, (((1,), (1,)), ((), ())), preferred_element_type=F32
    ).astype(BF16)
    returned = lax.all_to_all(
        grad_piece.reshape(tower_count, CAP, piece_rows), "tower", split_axis=0, concat_axis=0, tiled=True
    )
    returned = (
        returned.reshape(NGROUP, group_size, CAP, piece_rows)
        .transpose(0, 2, 1, 3)
        .reshape(NGROUP * CAP, model_width)
    )
    attn_grad = lax.dot_general(
        dispatch, returned, (((0,), (0,)), ((), ())), preferred_element_type=F32
    ).astype(BF16)

    def pairs(flip):
        return [(d, d ^ flip) for d in range(dp_count)]

    cot_parts = []
    for flip in range(dp_count):
        part = lax.dynamic_slice_in_dim(cot_rows, (dp_idx ^ flip) * piece_cols, piece_cols, 1)
        cot_parts.append(lax.ppermute(part, "dp", pairs(flip)) if flip else part)
    attn_parts = {0: attn_rows}
    flip = dp_count // 2
    while flip:
        for known in list(attn_parts):
            attn_parts[known ^ flip] = lax.ppermute(attn_parts[known], "dp", pairs(flip))
        flip //= 2
    weight_grad = weight_grad_of([attn_parts[flip] for flip in range(dp_count)], cot_parts)
    return (attn_grad, weight_grad)


def solution(mesh):
    return jax.shard_map(
        per_device,
        mesh=mesh,
        in_specs=(
            P(("dp", "tower"), None),
            P(("dp", "tower"), None),
            P(("dp", "tower")),
            P(),
            P("tower", None),
        ),
        out_specs=(P(("dp", "tower"), None), P("tower", "dp")),
        check_vma=False,
    )
```

time: 366 us -> 168 us (0.46)
  waiting for transfers between devices: 205 us -> 102 us
  blocking collectives: 79.2 us -> 0 us
  matrix products: 40 us -> 24.1 us
  Pallas kernels: 0 us -> 14.1 us
  between operations: 14.1 us -> 0.71 us
  starting transfers between devices: 7.45 us -> 18.5 us
  local copies, waits for them, and re-layouts: 14.6 us -> 3.62 us
    unnamed x2 -> x0, waiting for transfers between devices: 169 us -> none
    all_to_all x2 -> x0, blocking collectives: 79.2 us -> none  [the longest x1 40.6 us: per_device(): lax.all_to_all(cot_send, 'tower', split_axis=0, concat_axis=0, tiled=True)]
    all_to_all x0 -> x2, waiting for transfers between devices: none -> 67.9 us  [the longest x1 35.6 us: per_device(): lax.all_to_all(cot_send, 'tower', split_axis=0, concat_axis=0, tiled=True)]
    dot_general x5 -> x4, matrix products: 40 us -> 24.1 us  [the longest x1 18 us: per_device(): lax.dot_general(cot_rows, o_weight, (((1,), (1,)), ((), ())), preferred_e...]
    pallas_call x0 -> x1, Pallas kernels: none -> 14.1 us  [weight_grad_of(): pl.pallas_call(lambda *refs: weight_grad_kernel(count, *refs), grid=(feat...]
    unnamed x11 -> x6, local copies, waits for them, and re-layouts: 14.6 us -> 1.17 us
    all_to_all x0 -> x2, starting transfers between devices: none -> 7.28 us  [the longest x1 3.64 us: per_device(): lax.all_to_all(grad_piece.reshape(tower_count, CAP, piece_rows), 'tower',...]
    ppermute x0 -> x6, starting transfers between devices: none -> 3.95 us  [the longest x3 2.09 us: per_device(): lax.ppermute(attn_parts[known], 'dp', pairs(flip))]
  transfers between devices with their start and end apart: 2 -> 9, of which waited for: 2 -> 3; matrix products, arithmetic and copies ran while one was open for 6% -> 15% of each run, Pallas kernels for 0% -> 0%
where the time goes in v1:
time: 168 us
  waiting for transfers between devices  102 us (61%)
  matrix products  24.1 us (14%)
  starting transfers between devices  18.5 us (11%)
  Pallas kernels  14.1 us (8%)
  other arithmetic  4.47 us (3%)
  local copies, waits for them, and re-layouts  3.62 us (2%)
    all_to_all x1, waiting for transfers between devices, per_device(): lax.all_to_all(cot_send, 'tower', split_axis=0, concat_axis=0, tiled=True)  35.6 us
    all_to_all x1, waiting for transfers between devices, per_device(): lax.all_to_all(attn_send, 'tower', split_axis=0, concat_axis=0, tiled=True)  34.1 us
    all_to_all x1, waiting for transfers between devices, per_device(): lax.all_to_all(grad_piece.reshape(tower_count, CAP, piece_rows), 'tower',...  32.3 us
    dot_general x1, matrix products, per_device(): lax.dot_general(cot_rows, o_weight, (((1,), (1,)), ((), ())), preferred_e...  18 us
    pallas_call x1, Pallas kernels, weight_grad_of(): pl.pallas_call(lambda *refs: weight_grad_kernel(count, *refs), grid=(feat...  14.1 us
    all_to_all x1, starting transfers between devices, per_device(): lax.all_to_all(attn_send, 'tower', split_axis=0, concat_axis=0, tiled=True)  7.28 us
    all_to_all x1, starting transfers between devices, per_device(): lax.all_to_all(grad_piece.reshape(tower_count, CAP, piece_rows), 'tower',...  3.64 us
    all_to_all x1, starting transfers between devices, per_device(): lax.all_to_all(cot_send, 'tower', split_axis=0, concat_axis=0, tiled=True)  3.64 us
  transfers between devices with their start and end apart: 9, of which 3 were waited for; matrix products, arithmetic and copies ran while one was open for 15% of the time, Pallas kernels for 0%

profile of v1, /device:TPU:0, one launch (start us, length us, event | category | flops | bytes accessed | tf_op | source)
XLA Modules:
  0.0 167.6 jit_solution(16181020304650420290)
XLA Ops:
  0.6 0.0 copy-start
  0.6 0.7 fusion.4
  1.4 0.2 reduce_window_sum.22
  1.6 0.8 select_reduce_fusion.3
  2.4 0.7 fusion
  3.1 0.2 reduce_window_sum.23
  3.3 0.8 select_reduce_fusion
  4.1 0.1 and_select_fusion.1
  4.2 0.8 select_reduce_fusion.2
  5.0 0.1 fusion.6
  5.1 0.0 copy-done
  5.1 1.7 %convolution_convert_fusion = bf16[192,4096]{1,0:T(8,128)(2,1)} fusion(bf16[128,4096]{1,0:T(8,128)(2,1)S(1)} %copy-done, s32[128]{0:T(128)S(1)} %fusion.6), kind=kOutput, calls=%fused_computation | convolution fusion | flops 202137600 | bytes 2621952 | tf_op jit(solution)/shard_map/dot_general | solution.py:80
  6.9 7.3 %all-to-all-start.2 = ((bf16[8,24,4096]{2,1,0:T(8,128)(2,1)}), bf16[8,24,4096]{2,1,0:T(8,128)(2,1)S(1)}, u32[]{:S(2)}, u32[]{:S(2)}) async-start(bf16[8,24,4096]{2,1,0:T(8,128)(2,1)} %bitcast.4), calls=%async_computation.2 | async-start | bytes 3145728 | tf_op jit(solution)/shard_map/all_to_all | solution.py:90
  14.1 2.9 %convolution_convert_fusion.2 = bf16[192,4096]{1,0:T(8,128)(2,1)} fusion(bf16[128,4096]{1,0:T(8,128)(2,1)} %param.6, s32[128]{0:T(128)S(1)} %fusion.6), kind=kOutput, calls=%fused_computation.2 | convolution fusion | flops 202137600 | bytes 2621952 | tf_op jit(solution)/shard_map/dot_general | solution.py:79
  17.1 34.1 %all-to-all-done.2 = bf16[8,24,4096]{2,1,0:T(8,128)(2,1)S(1)} async-done(((bf16[8,24,4096]{2,1,0:T(8,128)(2,1)}), bf16[8,24,4096]{2,1,0:T(8,128)(2,1)S(1)}, u32[]{:S(2)}, u32[]{:S(2)}) %all-to-all-start.2) | async-done | bytes 1572896 | tf_op jit(solution)/shard_map/all_to_all | solution.py:90
  51.1 0.0 copy-start.2
  51.1 1.2 copy-done.2
  52.3 3.6 %all-to-all-start = ((bf16[8,24,4096]{2,1,0:T(8,128)(2,1)}), bf16[8,24,4096]{2,1,0:T(8,128)(2,1)S(1)}, u32[]{:S(2)}, u32[]{:S(2)}) async-start(bf16[8,24,4096]{2,1,0:T(8,128)(2,1)} %bitcast), calls=%async_computation | async-start | bytes 3145728 | tf_op jit(solution)/shard_map/all_to_all | solution.py:89
  55.9 1.6 collective-permute-start.1
  57.5 35.6 %all-to-all-done = bf16[8,24,4096]{2,1,0:T(8,128)(2,1)S(1)} async-done(((bf16[8,24,4096]{2,1,0:T(8,128)(2,1)}), bf16[8,24,4096]{2,1,0:T(8,128)(2,1)S(1)}, u32[]{:S(2)}, u32[]{:S(2)}) %all-to-all-start) | async-done | bytes 1572896 | tf_op jit(solution)/shard_map/all_to_all | solution.py:89
  93.1 0.0 copy-start.1
  93.1 18.0 %convolution_convert_fusion.1 = bf16[192,4096]{1,0:T(8,128)(2,1)} fusion(bf16[192,4096]{1,0:T(8,128)(2,1)S(1)} %bitcast.12, bf16[4096,4096]{1,0:T(8,128)(2,1)} %param.9), kind=kOutput, calls=%fused_computation.1 | convolution fusion | flops 6443237376 | bytes 36700160 | tf_op jit(solution)/shard_map/dot_general | solution.py:94
  111.2 0.0 copy-done.1
  111.2 3.6 %all-to-all-start.1 = ((bf16[8,24,4096]{2,1,0:T(8,128)(2,1)}), bf16[8,24,4096]{2,1,0:T(8,128)(2,1)S(1)}, u32[]{:S(2)}, u32[]{:S(2)}) async-start(bf16[8,24,4096]{2,1,0:T(8,128)(2,1)} %bitcast.17), calls=%async_computation.1 | async-start | bytes 3145728 | tf_op jit(solution)/shard_map/all_to_all | solution.py:97
  114.8 0.0 collective-permute-start
  114.9 0.0 collective-permute-done.1.refs_2_
  114.9 0.5 collective-permute-start.2
  115.4 2.5 %constant_dynamic-slice_fusion.2 = (bf16[192,1024]{1,0:T(8,128)(2,1)}, bf16[192,1024]{1,0:T(8,128)(2,1)S(1)}, bf16[192,1024]{1,0:T(8,128)(2,1)S(1)}, bf16[192,1024]{1,0:T(8,128)(2,1)}) fusion(bf16[192,4096]{1,0:T(8,128)(2,1)} %bitcast.13, s32[]{:T(128)S(6)} %select_n.43, s32[]{:T(128)S(6)} %select_n.42, s32[]{:T(128)S(6)} %select_n.41, s32[]{:T(128)S(6)} %select_n.40), kind=kLoop, calls=%fused_computation.22 | loop fusion | bytes 3145744 | tf_op jit(solution)/shard_map/dynamic_slice | solution.py:114
  117.8 1.2 collective-permute-start.5
  119.0 0.5 collective-permute-start.4
  119.5 0.1 collective-permute-start.3
  119.7 32.3 %all-to-all-done.1 = bf16[8,24,4096]{2,1,0:T(8,128)(2,1)S(1)} async-done(((bf16[8,24,4096]{2,1,0:T(8,128)(2,1)}), bf16[8,24,4096]{2,1,0:T(8,128)(2,1)S(1)}, u32[]{:S(2)}, u32[]{:S(2)}) %all-to-all-start.1) | async-done | bytes 1572896 | tf_op jit(solution)/shard_map/all_to_all | solution.py:97
  152.0 1.5 convolution_convert_fusion.3
  153.5 0.0 collective-permute-done.5.refs_7_
  153.5 0.0 collective-permute-done.4.refs_6_
  153.5 0.0 collective-permute-done.3.refs_5_
  153.5 0.0 collective-permute-done.refs_1_
  153.5 0.0 collective-permute-done.2.refs_3_
  153.5 14.1 %shard_map.68 = bf16[4096,1024]{1,0:T(8,128)(2,1)} custom-call(bf16[192,4096]{1,0:T(8,128)(2,1)} %bitcast.16, bf16[192,4096]{1,0:T(8,128)(2,1)} %collective-permute-done.refs_1_, bf16[192,4096]{1,0:T(8,128)(2,1)} %collective-permute-done.1.refs_2_, bf16[192,4096]{1,0:T(8,128)(2,1)} %collective-permute-done.2.refs_3_, ...), custom_call_target="tpu_custom_call" | custom-call | flops 6442450944 | bytes 16252928 | tf_op jit(solution)/shard_map/pallas_call | solution.py:49
Async XLA Ops:
  0.6 4.5 %copy-start = (bf16[128,4096]{1,0:T(8,128)(2,1)S(1)}, bf16[128,4096]{1,0:T(8,128)(2,1)}, u32[]{:S(2)}) copy-start(bf16[128,4096]{1,0:T(8,128)(2,1)} %param.5) | copy-start | bytes 3145732
  6.9 44.3 %all-to-all-start.2 = ((bf16[8,24,4096]{2,1,0:T(8,128)(2,1)}), bf16[8,24,4096]{2,1,0:T(8,128)(2,1)S(1)}, u32[]{:S(2)}, u32[]{:S(2)}) async-start(bf16[8,24,4096]{2,1,0:T(8,128)(2,1)} %bitcast.4), calls=%async_computation.2 | async-start | bytes 3145728 | tf_op jit(solution)/shard_map/all_to_all | solution.py:90
  51.1 1.2 copy-start.2
  52.3 40.8 %all-to-all-start = ((bf16[8,24,4096]{2,1,0:T(8,128)(2,1)}), bf16[8,24,4096]{2,1,0:T(8,128)(2,1)S(1)}, u32[]{:S(2)}, u32[]{:S(2)}) async-start(bf16[8,24,4096]{2,1,0:T(8,128)(2,1)} %bitcast), calls=%async_computation | async-start | bytes 3145728 | tf_op jit(solution)/shard_map/all_to_all | solution.py:89
  55.9 58.9 %collective-permute-start.1 = (bf16[192,4096]{1,0:T(8,128)(2,1)}, bf16[192,4096]{1,0:T(8,128)(2,1)}, u32[]{:S(2)}, u32[]{:S(2)}) collective-permute-start(bf16[192,4096]{1,0:T(8,128)(2,1)} %bitcast.14), channel_id=1, source_target_pairs={{0,16},{8,24},{16,0},{24,8},{1,17},{9,25},{17,1},{25,9},{2,18},{10... | collective-permute-start | bytes 4718600 | tf_op jit(solution)/shard_map/ppermute | solution.py:120
  93.1 18.0 %copy-start.1 = (bf16[8,24,4096]{2,1,0:T(8,128)(2,1)}, bf16[8,24,4096]{2,1,0:T(8,128)(2,1)S(1)}, u32[]{:S(2)}) copy-start(bf16[8,24,4096]{2,1,0:T(8,128)(2,1)S(1)} %all-to-all-done) | copy-start | bytes 4718596
  111.2 40.8 %all-to-all-start.1 = ((bf16[8,24,4096]{2,1,0:T(8,128)(2,1)}), bf16[8,24,4096]{2,1,0:T(8,128)(2,1)S(1)}, u32[]{:S(2)}, u32[]{:S(2)}) async-start(bf16[8,24,4096]{2,1,0:T(8,128)(2,1)} %bitcast.17), calls=%async_computation.1 | async-start | bytes 3145728 | tf_op jit(solution)/shard_map/all_to_all | solution.py:97
  114.8 38.7 %collective-permute-start = (bf16[192,4096]{1,0:T(8,128)(2,1)}, bf16[192,4096]{1,0:T(8,128)(2,1)}, u32[]{:S(2)}, u32[]{:S(2)}) collective-permute-start(bf16[192,4096]{1,0:T(8,128)(2,1)} %bitcast.15), channel_id=1, source_target_pairs={{0,8},{8,0},{16,24},{24,16},{1,9},{9,1},{17,25},{25,17},{2,10},{10... | collective-permute-start | bytes 4718600 | tf_op jit(solution)/shard_map/ppermute | solution.py:120
  114.9 38.6 %collective-permute-start.2 = (bf16[192,4096]{1,0:T(8,128)(2,1)}, bf16[192,4096]{1,0:T(8,128)(2,1)}, u32[]{:S(2)}, u32[]{:S(2)}) collective-permute-start(bf16[192,4096]{1,0:T(8,128)(2,1)} %collective-permute-done.1.refs_2_), channel_id=1, source_target_pairs={{0,8},{8,0},{16,24},{24,16},{1,9},{9,1},{17,25},{25,17},{2,10},{10... | collective-permute-start | bytes 4718600 | tf_op jit(solution)/shard_map/ppermute | solution.py:120
  117.8 35.6 %collective-permute-start.5 = (bf16[192,1024]{1,0:T(8,128)(2,1)}, bf16[192,1024]{1,0:T(8,128)(2,1)}, u32[]{:S(2)}, u32[]{:S(2)}) collective-permute-start(bf16[192,1024]{1,0:T(8,128)(2,1)} %get-tuple-element.6), channel_id=1, source_target_pairs={{0,24},{8,16},{16,8},{24,0},{1,25},{9,17},{17,9},{25,1},{2,26},{10... | collective-permute-start | bytes 1179656 | tf_op jit(solution)/shard_map/ppermute | solution.py:115
  119.0 34.4 %collective-permute-start.4 = (bf16[192,1024]{1,0:T(8,128)(2,1)S(1)}, bf16[192,1024]{1,0:T(8,128)(2,1)}, u32[]{:S(2)}, u32[]{:S(2)}) collective-permute-start(bf16[192,1024]{1,0:T(8,128)(2,1)S(1)} %get-tuple-element.7), channel_id=1, source_target_pairs={{0,16},{8,24},{16,0},{24,8},{1,17},{9,25},{17,1},{25,9},{2,18},{10... | collective-permute-start | bytes 1179656 | tf_op jit(solution)/shard_map/ppermute | solution.py:115
  119.5 33.9 %collective-permute-start.3 = (bf16[192,1024]{1,0:T(8,128)(2,1)S(1)}, bf16[192,1024]{1,0:T(8,128)(2,1)}, u32[]{:S(2)}, u32[]{:S(2)}) collective-permute-start(bf16[192,1024]{1,0:T(8,128)(2,1)S(1)} %get-tuple-element.8), channel_id=1, source_target_pairs={{0,8},{8,0},{16,24},{24,16},{1,9},{9,1},{17,25},{25,17},{2,10},{10... | collective-permute-start | bytes 1179656 | tf_op jit(solution)/shard_map/ppermute | solution.py:115

commit v2 on v1

v2 whole, which is shorter than its diff:
```python
import functools

import jax
import jax.numpy as jnp
from jax import lax
from jax.experimental import pallas as pl
from jax.experimental.pallas import tpu as pltpu
from jax.sharding import PartitionSpec as P


NGROUP = 8
KINDS = 3
CAP = 24
BF16 = jnp.bfloat16
F32 = jnp.float32
I32 = jnp.int32


MIB = 1 << 20


def grant(mib):
    return pltpu.CompilerParams(vmem_limit_bytes=mib * MIB)


def cost(flops, moved):
    return pl.CostEstimate(flops=flops, bytes_accessed=moved, transcendentals=0)


def dispatch_matrix(tower_idx, kinds_ref, modal_row):
    tokens = modal_row.shape[1]
    earlier = lax.broadcasted_iota(I32, (tokens, tokens), 0) < lax.broadcasted_iota(
        I32, (tokens, tokens), 1
    )
    kind_rows = lax.broadcasted_iota(I32, (8, tokens), 0)
    member = jnp.where(kind_rows == modal_row, 1.0, 0.0)
    before = jnp.dot(
        member.astype(BF16),
        jnp.where(earlier, 1.0, 0.0).astype(BF16),
        preferred_element_type=F32,
    )
    order_in = jnp.sum(member * before, axis=0, keepdims=True)
    kinds = [kinds_ref[g] for g in range(NGROUP)]
    seen = [jnp.int32(0)] * KINDS
    ranks = []
    for g in range(NGROUP):
        rank = jnp.int32(0)
        for m in range(KINDS):
            hit = kinds[g] == m
            rank = jnp.where(hit, seen[m], rank)
            seen[m] = seen[m] + jnp.where(hit, 1, 0)
        ranks.append(rank)
    how_many = jnp.zeros((1, tokens), F32)
    for m in range(KINDS):
        how_many = jnp.where(modal_row == m, seen[m].astype(F32), how_many)
    inverse = 1.0 / jnp.maximum(how_many, 1.0)
    slot_idx = jnp.floor((order_in + 0.5) * inverse)
    shifted = order_in + tower_idx.astype(F32)
    target = shifted - how_many * jnp.floor((shifted + 0.5) * inverse)
    target = target.astype(I32)
    block = jnp.zeros((1, tokens), I32)
    for g in range(NGROUP):
        chosen = (modal_row == kinds[g]) & (target == ranks[g])
        block = jnp.where(chosen, jnp.bitwise_xor(jnp.int32(g), tower_idx), block)
    place = block * CAP + slot_idx.astype(I32)
    slots = lax.broadcasted_iota(I32, (NGROUP * CAP, tokens), 0)
    return jnp.where(slots == place, 1.0, 0.0).astype(BF16)


def first_dispatch_kernel(tower_ref, kinds_ref, modal_ref, rows_ref, one_hot_ref, *out_refs):
    @pl.when(pl.program_id(0) == 0)
    def _():
        one_hot_ref[...] = dispatch_matrix(tower_ref[0], kinds_ref, modal_ref[...])

    dispatch_kernel(one_hot_ref, rows_ref, *out_refs)


def dispatch_kernel(one_hot_ref, rows_ref, *out_refs):
    placed = jnp.dot(one_hot_ref[...], rows_ref[...], preferred_element_type=F32)
    for k, out_ref in enumerate(out_refs):
        out_ref[...] = placed[k * CAP : (k + 1) * CAP, :].astype(BF16)


def dispatch_first(tower_idx, kinds, modal_row, rows):
    tokens, width = rows.shape
    block = min(1024, width)
    slots = NGROUP * CAP
    out = pl.pallas_call(
        first_dispatch_kernel,
        grid=(width // block,),
        in_specs=[
            pl.BlockSpec(memory_space=pltpu.SMEM),
            pl.BlockSpec(memory_space=pltpu.SMEM),
            pl.BlockSpec((1, tokens), lambda i: (0, 0)),
            pl.BlockSpec((tokens, block), lambda i: (0, i)),
        ],
        out_specs=[pl.BlockSpec((slots, tokens), lambda i: (0, 0))]
        + [pl.BlockSpec((CAP, block), lambda i: (0, i))] * NGROUP,
        out_shape=[jax.ShapeDtypeStruct((slots, tokens), BF16)]
        + [jax.ShapeDtypeStruct((CAP, width), BF16)] * NGROUP,
        cost_estimate=cost(2 * slots * tokens * width, 2 * (tokens + slots) * width),
        compiler_params=grant(56),
        name="dispatch_cot",
    )(tower_idx, kinds, modal_row, rows)
    return out[0], list(out[1:])


def dispatch_next(one_hot, rows):
    tokens, width = rows.shape
    block = min(1024, width)
    slots = one_hot.shape[0]
    return list(
        pl.pallas_call(
            dispatch_kernel,
            grid=(width // block,),
            in_specs=[
                pl.BlockSpec((slots, tokens), lambda i: (0, 0)),
                pl.BlockSpec((tokens, block), lambda i: (0, i)),
            ],
            out_specs=[pl.BlockSpec((CAP, block), lambda i: (0, i))] * NGROUP,
            out_shape=[jax.ShapeDtypeStruct((CAP, width), BF16)] * NGROUP,
            cost_estimate=cost(2 * slots * tokens * width, 2 * (tokens + slots) * width),
            compiler_params=grant(12),
            name="dispatch_attn",
        )(one_hot, rows)
    )


def pieces_kernel(dp_ref, *refs):
    block_refs, out_refs = refs[:NGROUP], refs[NGROUP:]
    columns = out_refs[0].shape[1]
    for f, out_ref in enumerate(out_refs):
        first = pl.multiple_of(jnp.bitwise_xor(dp_ref[0], jnp.int32(f)) * columns, 128)
        for k, block_ref in enumerate(block_refs):
            out_ref[k * CAP : (k + 1) * CAP, :] = block_ref[:, pl.ds(first, columns)]


def column_pieces(dp_idx, blocks):
    pieces = lax.axis_size("dp")
    width = blocks[0].shape[1]
    slots = NGROUP * CAP
    whole = pl.BlockSpec(memory_space=pltpu.VMEM)
    return pl.pallas_call(
        pieces_kernel,
        in_specs=[pl.BlockSpec(memory_space=pltpu.SMEM)] + [whole] * NGROUP,
        out_specs=[whole] * pieces,
        out_shape=[jax.ShapeDtypeStruct((slots, width // pieces), BF16)] * pieces,
        cost_estimate=cost(0, 4 * slots * width),
        compiler_params=grant(8),
        name="column_pieces",
    )(dp_idx, *blocks)


def token_grad_kernel(pieces, dp_ref, *refs):
    cot_refs, weight_refs, out_refs = refs[:pieces], refs[pieces : 2 * pieces], refs[2 * pieces :]
    grads = None
    for cot_ref, weight_ref in zip(cot_refs, weight_refs):
        term = lax.dot_general(
            cot_ref[...], weight_ref[...], (((1,), (1,)), ((), ())), preferred_element_type=F32
        )
        grads = term if grads is None else grads + term
    for k, out_ref in enumerate(out_refs):
        out_ref[...] = grads[k * CAP : (k + 1) * CAP, :].astype(BF16)


def token_grad(dp_idx, cot_pieces, weight):
    features, width = weight.shape
    pieces = len(cot_pieces)
    slots, columns = cot_pieces[0].shape
    block = min(512, features)

    def weight_spec(f):
        return pl.BlockSpec((block, columns), lambda i, dp_ref: (i, jnp.bitwise_xor(dp_ref[0], f)))

    return list(
        pl.pallas_call(
            functools.partial(token_grad_kernel, pieces),
            grid_spec=pltpu.PrefetchScalarGridSpec(
                num_scalar_prefetch=1,
                grid=(features // block,),
                in_specs=[pl.BlockSpec((slots, columns), lambda i, dp_ref: (0, 0))] * pieces
                + [weight_spec(f) for f in range(pieces)],
                out_specs=[pl.BlockSpec((CAP, block), lambda i, dp_ref: (0, i))] * NGROUP,
            ),
            out_shape=[jax.ShapeDtypeStruct((CAP, features), BF16)] * NGROUP,
            cost_estimate=cost(
                2 * slots * features * width, 2 * (features * width + 2 * slots * width)
            ),
            compiler_params=grant(20),
            name="token_grad",
        )(dp_idx, *cot_pieces, *[weight] * pieces)
    )


def combine_kernel(one_hot_ref, *refs):
    got_refs, out_ref, rows_ref = refs[:NGROUP], refs[NGROUP], refs[NGROUP + 1]
    for k, got_ref in enumerate(got_refs):
        rows_ref[k * CAP : (k + 1) * CAP, :] = got_ref[...]
    out_ref[...] = lax.dot_general(
        one_hot_ref[...], rows_ref[...], (((0,), (0,)), ((), ())), preferred_element_type=F32
    ).astype(BF16)


def combine(one_hot, blocks):
    slots, tokens = one_hot.shape
    width = blocks[0].shape[1]
    block = min(1024, width)
    return pl.pallas_call(
        combine_kernel,
        grid=(width // block,),
        in_specs=[pl.BlockSpec((slots, tokens), lambda i: (0, 0))]
        + [pl.BlockSpec((CAP, block), lambda i: (0, i))] * NGROUP,
        out_specs=pl.BlockSpec((tokens, block), lambda i: (0, i)),
        out_shape=jax.ShapeDtypeStruct((tokens, width), BF16),
        scratch_shapes=[pltpu.VMEM((slots, block), BF16)],
        cost_estimate=cost(2 * slots * tokens * width, 2 * (tokens + slots) * width),
        compiler_params=grant(8),
        name="combine",
    )(one_hot, *blocks)


def join_kernel(*refs):
    at = 0
    for ref in refs[:-1]:
        rows = ref.shape[0]
        refs[-1][at : at + rows, :] = ref[...]
        at += rows


def join_rows(blocks):
    rows = sum(block.shape[0] for block in blocks)
    width = blocks[0].shape[1]
    whole = pl.BlockSpec(memory_space=pltpu.VMEM)
    return pl.pallas_call(
        join_kernel,
        in_specs=[whole] * len(blocks),
        out_specs=whole,
        out_shape=jax.ShapeDtypeStruct((rows, width), BF16),
        cost_estimate=cost(0, 4 * rows * width),
        compiler_params=grant(8),
        name="join_rows",
    )(*blocks)


def weight_grad_kernel(n_attn, n_cot, *refs):
    attn_refs, cot_refs = refs[:n_attn], refs[n_attn : n_attn + n_cot]
    out_ref, attn_rows_ref, cot_rows_ref = refs[n_attn + n_cot :]

    @pl.when(pl.program_id(0) == 0)
    def _():
        at = 0
        for cot_ref in cot_refs:
            rows = cot_ref.shape[0]
            cot_rows_ref[at : at + rows, :] = cot_ref[...]
            at += rows

    at = 0
    for attn_ref in attn_refs:
        rows = attn_ref.shape[0]
        attn_rows_ref[at : at + rows, :] = attn_ref[...]
        at += rows
    out_ref[...] = lax.dot_general(
        attn_rows_ref[...],
        cot_rows_ref[...],
        (((0,), (0,)), ((), ())),
        preferred_element_type=F32,
    ).astype(out_ref.dtype)


def weight_grad_of(attn_parts, cot_parts):
    features = attn_parts[0].shape[1]
    columns = cot_parts[0].shape[1]
    rows = sum(part.shape[0] for part in attn_parts)
    block = min(512, features)
    return pl.pallas_call(
        functools.partial(weight_grad_kernel, len(attn_parts), len(cot_parts)),
        grid=(features // block,),
        in_specs=[pl.BlockSpec((part.shape[0], block), lambda i: (0, i)) for part in attn_parts]
        + [pl.BlockSpec((part.shape[0], columns), lambda i: (0, 0)) for part in cot_parts],
        out_specs=pl.BlockSpec((block, columns), lambda i: (i, 0)),
        out_shape=jax.ShapeDtypeStruct((features, columns), BF16),
        scratch_shapes=[pltpu.VMEM((rows, block), BF16), pltpu.VMEM((rows, columns), BF16)],
        cost_estimate=cost(
            2 * rows * features * columns, 2 * (rows * (features + columns) + features * columns)
        ),
        compiler_params=grant(20),
        name="weight_grad",
    )(*attn_parts, *cot_parts)


def flip_over(axis, value, flip):
    size = lax.axis_size(axis)
    return lax.ppermute(value, axis, [(i, i ^ flip) for i in range(size)])


def swap_blocks(blocks, order):
    got = {0: blocks[0]}
    for k in order:
        got[k] = flip_over("tower", blocks[k], k)
    return [got[k] for k in range(len(blocks))]


def gather_flips(value):
    parts = {0: value}
    flip = lax.axis_size("dp") // 2
    while flip:
        for known in list(parts):
            parts[known ^ flip] = flip_over("dp", parts[known], flip)
        flip //= 2
    return parts


FAR = (6, 7, 4, 5)
NEAR = (2, 3, 1)
LOWER = (0, 1, 2, 3)
UPPER = (4, 5, 6, 7)


def small_towers(attn_out, out_cot, modality, group_modality, o_weight):
    tower_idx = lax.axis_index("tower").astype(I32)
    dp_idx = lax.axis_index("dp").astype(I32).reshape(1)
    dp_count = lax.axis_size("dp")

    one_hot, cot_blocks = dispatch_first(
        tower_idx.reshape(1), group_modality, modality.reshape(1, -1), out_cot
    )
    attn_blocks = dispatch_next(one_hot, attn_out)
    cot_got = swap_blocks(cot_blocks, FAR + NEAR)
    attn_got = swap_blocks(attn_blocks, NEAR + FAR)
    cot_pieces = column_pieces(dp_idx, cot_got)
    cot_parts = [
        flip_over("dp", piece, flip) if flip else piece
        for flip, piece in enumerate(cot_pieces)
    ]
    grads = token_grad(dp_idx, cot_pieces, o_weight)
    returned = swap_blocks(grads, FAR + NEAR)
    attn_grad = combine(one_hot, returned)

    lower = join_rows([attn_got[k] for k in LOWER])
    upper = join_rows([attn_got[k] for k in UPPER])
    lower = gather_flips(lower)
    upper = gather_flips(upper)
    attn_parts = []
    for flip in range(dp_count):
        attn_parts += [lower[flip], upper[flip]]
    return attn_grad, weight_grad_of(attn_parts, cot_parts)


def large_towers(attn_out, out_cot, modality, group_modality, o_weight):
    tower_idx = lax.axis_index("tower").astype(I32)
    tower_count = lax.axis_size("tower")
    dp_idx = lax.axis_index("dp")
    dp_count = lax.axis_size("dp")
    group_size = tower_count // NGROUP
    piece_rows, width = o_weight.shape
    tokens = attn_out.shape[0]
    piece_cols = width // dp_count
    modal_row = modality.reshape(1, tokens)
    group_ids = jnp.arange(NGROUP, dtype=I32)
    member = modal_row == jnp.arange(KINDS, dtype=I32)[:, None]
    before = jnp.cumsum(member.astype(I32), axis=1) - 1
    order_in = jnp.sum(jnp.where(member, before, 0), axis=0)
    group_of = (group_modality[:, None] == jnp.arange(KINDS, dtype=I32)[None, :]).astype(I32)
    group_rank = jnp.sum((jnp.cumsum(group_of, axis=0) - group_of) * group_of, axis=1)
    how_many = jnp.sum(member * jnp.sum(group_of, axis=0)[:, None], axis=0)
    target = (order_in + tower_idx) % how_many
    chosen = (group_modality[:, None] == modal_row) & (group_rank[:, None] == target[None, :])
    routed = jnp.sum(chosen.astype(I32) * group_ids[:, None], axis=0)
    place = routed * CAP + order_in // how_many
    one_hot = (place[None, :] == jnp.arange(NGROUP * CAP, dtype=I32)[:, None]).astype(BF16)

    def swap(value):
        return lax.all_to_all(value, "tower", split_axis=0, concat_axis=0, tiled=True)

    cot_group = jnp.dot(one_hot, out_cot, preferred_element_type=F32).astype(BF16)
    attn_group = jnp.dot(one_hot, attn_out, preferred_element_type=F32).astype(BF16)
    cot_send = jnp.broadcast_to(
        cot_group.reshape(NGROUP, 1, CAP, width), (NGROUP, group_size, CAP, width)
    ).reshape(tower_count, CAP, width)
    attn_send = (
        attn_group.reshape(NGROUP, CAP, group_size, piece_rows)
        .transpose(0, 2, 1, 3)
        .reshape(tower_count, CAP, piece_rows)
    )
    cot_rows = swap(cot_send).reshape(tower_count * CAP, width)
    attn_rows = swap(attn_send).reshape(tower_count * CAP, piece_rows)
    grads = lax.dot_general(
        cot_rows, o_weight, (((1,), (1,)), ((), ())), preferred_element_type=F32
    ).astype(BF16)
    returned = (
        swap(grads.reshape(tower_count, CAP, piece_rows))
        .reshape(NGROUP, group_size, CAP, piece_rows)
        .transpose(0, 2, 1, 3)
        .reshape(NGROUP * CAP, width)
    )
    attn_grad = lax.dot_general(
        one_hot, returned, (((0,), (0,)), ((), ())), preferred_element_type=F32
    ).astype(BF16)
    cot_parts = []
    for flip in range(dp_count):
        part = lax.dynamic_slice_in_dim(cot_rows, (dp_idx ^ flip) * piece_cols, piece_cols, 1)
        cot_parts.append(flip_over("dp", part, flip) if flip else part)
    attn_parts = gather_flips(attn_rows)
    return attn_grad, weight_grad_of([attn_parts[flip] for flip in range(dp_count)], cot_parts)


def per_device(*args):
    if lax.axis_size("tower") == NGROUP:
        return small_towers(*args)
    return large_towers(*args)


def solution(mesh):
    return jax.shard_map(
        per_device,
        mesh=mesh,
        in_specs=(
            P(("dp", "tower"), None),
            P(("dp", "tower"), None),
            P(("dp", "tower")),
            P(),
            P("tower", None),
        ),
        out_specs=(P(("dp", "tower"), None), P("tower", "dp")),
        check_vma=False,
    )
```

time: 168 us -> 166 us (0.988)
  starting transfers between devices: 18.5 us -> 61.9 us
  waiting for transfers between devices: 102 us -> 65 us
  matrix products: 24.1 us -> 0 us
  Pallas kernels: 14.1 us -> 35.1 us
  other arithmetic: 4.47 us -> 0 us
    all_to_all x3 -> x0, waiting for transfers between devices: 102 us -> none  [the longest x1 35.6 us: per_device(): lax.all_to_all(cot_send, 'tower', split_axis=0, concat_axis=0, tiled=True)]
    ppermute x6 -> x30, waiting for transfers between devices: 0.02 us -> 65 us  [flip_over(): return lax.ppermute(value, axis, [(i, i ^ flip) for i in range(size)])]
    ppermute x6 -> x30, starting transfers between devices: 3.95 us -> 61.9 us  [flip_over(): return lax.ppermute(value, axis, [(i, i ^ flip) for i in range(size)])]
    dot_general x4 -> x0, matrix products: 24.1 us -> none  [the longest x1 18 us: per_device(): lax.dot_general(cot_rows, o_weight, (((1,), (1,)), ((), ())), preferred_e...]
    pallas_call x1 -> x8, Pallas kernels: 14.1 us -> 35.1 us  [the longest x1 17.3 us: token_grad(): pl.pallas_call(functools.partial(token_grad_kernel, pieces), grid_spec=pl...]
    all_to_all x3 -> x0, starting transfers between devices: 14.6 us -> none  [the longest x1 7.28 us: per_device(): lax.all_to_all(attn_send, 'tower', split_axis=0, concat_axis=0, tiled=True)]
    dynamic_slice x1 -> x0, local copies, waits for them, and re-layouts: 2.45 us -> none  [per_device(): lax.dynamic_slice_in_dim(cot_rows, (dp_idx ^ flip) * piece_cols, piece_co...]
    reduce_sum x3 -> x0, other arithmetic: 2.37 us -> none  [the longest x1 0.83 us: routing(): how_many = jnp.sum(member * per_kind[None, :], axis=1)]
  transfers between devices with their start and end apart: 9 -> 30, of which waited for: 3 -> 13; matrix products, arithmetic and copies ran while one was open for 15% -> 0% of each run, Pallas kernels for 0% -> 13%
where the time goes in v2:
time: 166 us
  waiting for transfers between devices  65 us (39%)
  starting transfers between devices  61.9 us (37%)
  Pallas kernels  35.1 us (21%)
  local copies, waits for them, and re-layouts  2.95 us (2%)
    ppermute x30, waiting for transfers between devices, flip_over(): return lax.ppermute(value, axis, [(i, i ^ flip) for i in range(size)])  65 us
    ppermute x30, starting transfers between devices, flip_over(): return lax.ppermute(value, axis, [(i, i ^ flip) for i in range(size)])  61.9 us
    pallas_call x1, Pallas kernels, token_grad(): pl.pallas_call(functools.partial(token_grad_kernel, pieces), grid_spec=pl...  17.3 us
    pallas_call x1, Pallas kernels, weight_grad_of(): pl.pallas_call(functools.partial(weight_grad_kernel, len(attn_parts), len...  10 us
    pallas_call x1, Pallas kernels, dispatch_first(): pl.pallas_call(first_dispatch_kernel, grid=(width // block,), in_specs=[p...  4.05 us
  transfers between devices with their start and end apart: 30, of which 13 were waited for; matrix products, arithmetic and copies ran while one was open for 0% of the time, Pallas kernels for 13%

profile of v2, /device:TPU:0, one launch (start us, length us, event | category | flops | bytes accessed | tf_op | source)
XLA Modules:
  0.0 165.7 jit_solution(13823441128910800173)
XLA Ops:
  0.6 4.0 %dispatch_cot.1 = (bf16[192,128]{1,0:T(8,128)(2,1)}, bf16[24,4096]{1,0:T(8,128)(2,1)}, bf16[24,4096]{1,0:T(8,128)(2,1)}, bf16[24,4096]{1,0:T(8,128)(2,1)}, bf16[...) custom-call(s32[1]{0:T(128)} %bitcast.tower_ref, ...), custom_call_target="tpu_custom_call" | custom-call | flops 201326592 | bytes 2621440 | tf_op jit(solution)/shard_map/dispatch_cot/pallas_call | solution.py:88
  4.7 3.0 %collective-permute-start = (bf16[24,4096]{1,0:T(8,128)(2,1)}, bf16[24,4096]{1,0:T(8,128)(2,1)S(1)}, u32[]{:S(2)}, u32[]{:S(2)}) collective-permute-start(bf16[24,4096]{1,0:T(8,128)(2,1)} %get-tuple-element.33), channel_id=1, source_target_pairs={{0,1},{1,0},{2,3},{3,2},{4,5},{5,4},{6,7},{7,6},{8,9},{9,8},{10,11... | collective-permute-start | bytes 589832 | tf_op jit(solution)/shard_map/ppermute | solution.py:293
  7.7 1.6 collective-permute-start.1
  9.3 1.2 copy-done
  10.5 0.8 copy-done.2
  11.3 1.2 dispatch_attn.1
  12.6 0.6 collective-permute-start.14
  13.2 0.0 collective-permute-start.15
  13.2 2.9 %collective-permute-start.16 = (bf16[24,4096]{1,0:T(8,128)(2,1)S(1)}, bf16[24,4096]{1,0:T(8,128)(2,1)S(1)}, u32[]{:S(2)}, u32[]{:S(2)}) collective-permute-start(bf16[24,4096]{1,0:T(8,128)(2,1)S(1)} %get-tuple-element.55), channel_id=1, source_target_pairs={{0,3},{1,2},{2,1},{3,0},{4,7},{5,6},{6,5},{7,4},{8,11},{9,10},{10,... | collective-permute-start | bytes 589832 | tf_op jit(solution)/shard_map/ppermute | solution.py:293
  16.1 0.0 collective-permute-done.refs_1_
  16.1 2.6 %collective-permute-start.17 = (bf16[24,4096]{1,0:T(8,128)(2,1)S(1)}, bf16[24,4096]{1,0:T(8,128)(2,1)S(1)}, u32[]{:S(2)}, u32[]{:S(2)}) collective-permute-start(bf16[24,4096]{1,0:T(8,128)(2,1)S(1)} %get-tuple-element.56), channel_id=1, source_target_pairs={{0,4},{1,5},{2,6},{3,7},{4,0},{5,1},{6,2},{7,3},{8,12},{9,13},{10,... | collective-permute-start | bytes 589832 | tf_op jit(solution)/shard_map/ppermute | solution.py:293
  18.7 0.0 collective-permute-done.1.refs_2_
  18.7 0.3 collective-permute-start.18
  19.0 0.0 collective-permute-done.14.refs_1_
  19.0 2.5 %collective-permute-start.19 = (bf16[24,4096]{1,0:T(8,128)(2,1)S(1)}, bf16[24,4096]{1,0:T(8,128)(2,1)S(1)}, u32[]{:S(2)}, u32[]{:S(2)}) collective-permute-start(bf16[24,4096]{1,0:T(8,128)(2,1)S(1)} %get-tuple-element.58), channel_id=1, source_target_pairs={{0,6},{1,7},{2,4},{3,5},{4,2},{5,3},{6,0},{7,1},{8,14},{9,15},{10,... | collective-permute-start | bytes 589832 | tf_op jit(solution)/shard_map/ppermute | solution.py:293
  21.5 6.0 %collective-permute-done.15.refs_2_ = bf16[24,4096]{1,0:T(8,128)(2,1)S(1)} collective-permute-done((bf16[24,4096]{1,0:T(8,128)(2,1)S(1)}, bf16[24,4096]{1,0:T(8,128)(2,1)S(1)}, u32[]{:S(2)}, u32[]{:S(2)}) %collective-permute-start.15) | collective-permute-done | bytes 196640 | tf_op jit(solution)/shard_map/ppermute | solution.py:293
  27.5 2.7 %collective-permute-start.20 = (bf16[24,4096]{1,0:T(8,128)(2,1)S(1)}, bf16[24,4096]{1,0:T(8,128)(2,1)S(1)}, u32[]{:S(2)}, u32[]{:S(2)}) collective-permute-start(bf16[24,4096]{1,0:T(8,128)(2,1)S(1)} %get-tuple-element.59), channel_id=1, source_target_pairs={{0,7},{1,6},{2,5},{3,4},{4,3},{5,2},{6,1},{7,0},{8,15},{9,14},{10,... | collective-permute-start | bytes 589832 | tf_op jit(solution)/shard_map/ppermute | solution.py:293
  30.3 1.2 collective-permute-done.16.refs_3_
  31.5 0.0 collective-permute-start.2
  31.5 0.0 collective-permute-done.17.refs_0_
  31.5 1.9 %collective-permute-start.3 = (bf16[24,4096]{1,0:T(8,128)(2,1)}, bf16[24,4096]{1,0:T(8,128)(2,1)S(1)}, u32[]{:S(2)}, u32[]{:S(2)}) collective-permute-start(bf16[24,4096]{1,0:T(8,128)(2,1)} %get-tuple-element.36), channel_id=1, source_target_pairs={{0,4},{1,5},{2,6},{3,7},{4,0},{5,1},{6,2},{7,3},{8,12},{9,13},{10,... | collective-permute-start | bytes 589832 | tf_op jit(solution)/shard_map/ppermute | solution.py:293
  33.4 11.8 %collective-permute-done.18.refs_1_ = bf16[24,4096]{1,0:T(8,128)(2,1)S(1)} collective-permute-done((bf16[24,4096]{1,0:T(8,128)(2,1)S(1)}, bf16[24,4096]{1,0:T(8,128)(2,1)S(1)}, u32[]{:S(2)}, u32[]{:S(2)}) %collective-permute-start.18) | collective-permute-done | bytes 196640 | tf_op jit(solution)/shard_map/ppermute | solution.py:293
  45.2 0.0 collective-permute-done.19.refs_2_
  45.2 15.8 %collective-permute-start.5 = (bf16[24,4096]{1,0:T(8,128)(2,1)}, bf16[24,4096]{1,0:T(8,128)(2,1)S(1)}, u32[]{:S(2)}, u32[]{:S(2)}) collective-permute-start(bf16[24,4096]{1,0:T(8,128)(2,1)} %get-tuple-element.38), channel_id=1, source_target_pairs={{0,6},{1,7},{2,4},{3,5},{4,2},{5,3},{6,0},{7,1},{8,14},{9,15},{10,... | collective-permute-start | bytes 589832 | tf_op jit(solution)/shard_map/ppermute | solution.py:293
  61.0 0.0 collective-permute-done.20.refs_3_
  61.0 1.0 collective-permute-start.6
  62.0 0.1 join_rows.2.refs_0_
  62.1 0.1 join_rows.3.refs_1_
  62.1 0.0 collective-permute-done.2.refs_3_
  62.1 1.6 collective-permute-start.24
  63.7 11.7 %collective-permute-done.3.refs_4_ = bf16[24,4096]{1,0:T(8,128)(2,1)S(1)} collective-permute-done((bf16[24,4096]{1,0:T(8,128)(2,1)}, bf16[24,4096]{1,0:T(8,128)(2,1)S(1)}, u32[]{:S(2)}, u32[]{:S(2)}) %collective-permute-start.3) | collective-permute-done | bytes 196640 | tf_op jit(solution)/shard_map/ppermute | solution.py:293
  75.4 1.5 collective-permute-start.23
  76.9 2.0 %collective-permute-done.4.refs_5_ = bf16[24,4096]{1,0:T(8,128)(2,1)S(1)} collective-permute-done((bf16[24,4096]{1,0:T(8,128)(2,1)}, bf16[24,4096]{1,0:T(8,128)(2,1)S(1)}, u32[]{:S(2)}, u32[]{:S(2)}) %collective-permute-start.4) | collective-permute-done | bytes 196640 | tf_op jit(solution)/shard_map/ppermute | solution.py:293
  78.9 0.0 collective-permute-done.5.refs_6_
  78.9 0.9 copy-done.1
  79.8 0.1 column_pieces.1
  79.9 17.3 %token_grad.1 = (bf16[24,4096]{1,0:T(8,128)(2,1)S(1)}, bf16[24,4096]{1,0:T(8,128)(2,1)S(1)}, bf16[24,4096]{1,0:T(8,128)(2,1)S(1)}, bf16[24,4096]{1,0:T(8,128)(2,...) custom-call(s32[1]{0:T(128)} %bitcast.2.dp_ref, ...), custom_call_target="tpu_custom_call" | custom-call | flops 6442450944 | bytes 36700160 | tf_op jit(solution)/shard_map/token_grad/pallas_call | solution.py:176
  97.2 2.3 %collective-permute-start.7 = (bf16[24,4096]{1,0:T(8,128)(2,1)S(1)}, bf16[24,4096]{1,0:T(8,128)(2,1)S(1)}, u32[]{:S(2)}, u32[]{:S(2)}) collective-permute-start(bf16[24,4096]{1,0:T(8,128)(2,1)S(1)} %get-tuple-element.45), channel_id=1, source_target_pairs={{0,1},{1,0},{2,3},{3,2},{4,5},{5,4},{6,7},{7,6},{8,9},{9,8},{10,11... | collective-permute-start | bytes 589832 | tf_op jit(solution)/shard_map/ppermute | solution.py:293
  99.5 6.6 %collective-permute-start.8 = (bf16[24,4096]{1,0:T(8,128)(2,1)S(1)}, bf16[24,4096]{1,0:T(8,128)(2,1)S(1)}, u32[]{:S(2)}, u32[]{:S(2)}) collective-permute-start(bf16[24,4096]{1,0:T(8,128)(2,1)S(1)} %get-tuple-element.46), channel_id=1, source_target_pairs={{0,2},{1,3},{2,0},{3,1},{4,6},{5,7},{6,4},{7,5},{8,10},{9,11},{10,... | collective-permute-start | bytes 589832 | tf_op jit(solution)/shard_map/ppermute | solution.py:293
  106.1 0.2 collective-permute-start.9
  106.3 0.0 collective-permute-done.7.refs_1_
  106.3 6.6 %collective-permute-start.10 = (bf16[24,4096]{1,0:T(8,128)(2,1)S(1)}, bf16[24,4096]{1,0:T(8,128)(2,1)S(1)}, u32[]{:S(2)}, u32[]{:S(2)}) collective-permute-start(bf16[24,4096]{1,0:T(8,128)(2,1)S(1)} %get-tuple-element.48), channel_id=1, source_target_pairs={{0,4},{1,5},{2,6},{3,7},{4,0},{5,1},{6,2},{7,3},{8,12},{9,13},{10,... | collective-permute-start | bytes 589832 | tf_op jit(solution)/shard_map/ppermute | solution.py:293
  112.9 2.4 %collective-permute-done.8.refs_2_ = bf16[24,4096]{1,0:T(8,128)(2,1)S(1)} collective-permute-done((bf16[24,4096]{1,0:T(8,128)(2,1)S(1)}, bf16[24,4096]{1,0:T(8,128)(2,1)S(1)}, u32[]{:S(2)}, u32[]{:S(2)}) %collective-permute-start.8) | collective-permute-done | bytes 196640 | tf_op jit(solution)/shard_map/ppermute | solution.py:293
  115.3 0.0 collective-permute-start.11
  115.3 4.1 %collective-permute-done.9.refs_3_ = bf16[24,4096]{1,0:T(8,128)(2,1)S(1)} collective-permute-done((bf16[24,4096]{1,0:T(8,128)(2,1)S(1)}, bf16[24,4096]{1,0:T(8,128)(2,1)S(1)}, u32[]{:S(2)}, u32[]{:S(2)}) %collective-permute-start.9) | collective-permute-done | bytes 196640 | tf_op jit(solution)/shard_map/ppermute | solution.py:293
  119.4 9.6 %collective-permute-done.10.refs_4_ = bf16[24,4096]{1,0:T(8,128)(2,1)S(1)} collective-permute-done((bf16[24,4096]{1,0:T(8,128)(2,1)S(1)}, bf16[24,4096]{1,0:T(8,128)(2,1)S(1)}, u32[]{:S(2)}, u32[]{:S(2)}) %collective-permute-start.10) | collective-permute-done | bytes 196640 | tf_op jit(solution)/shard_map/ppermute | solution.py:293
  129.0 2.4 %collective-permute-start.12 = (bf16[24,4096]{1,0:T(8,128)(2,1)S(1)}, bf16[24,4096]{1,0:T(8,128)(2,1)S(1)}, u32[]{:S(2)}, u32[]{:S(2)}) collective-permute-start(bf16[24,4096]{1,0:T(8,128)(2,1)S(1)} %get-tuple-element.50), channel_id=1, source_target_pairs={{0,6},{1,7},{2,4},{3,5},{4,2},{5,3},{6,0},{7,1},{8,14},{9,15},{10,... | collective-permute-start | bytes 589832 | tf_op jit(solution)/shard_map/ppermute | solution.py:293
  131.4 1.9 %collective-permute-done.11.refs_5_ = bf16[24,4096]{1,0:T(8,128)(2,1)S(1)} collective-permute-done((bf16[24,4096]{1,0:T(8,128)(2,1)S(1)}, bf16[24,4096]{1,0:T(8,128)(2,1)S(1)}, u32[]{:S(2)}, u32[]{:S(2)}) %collective-permute-start.11) | collective-permute-done | bytes 196640 | tf_op jit(solution)/shard_map/ppermute | solution.py:293
  133.3 3.2 %collective-permute-start.13 = (bf16[24,4096]{1,0:T(8,128)(2,1)S(1)}, bf16[24,4096]{1,0:T(8,128)(2,1)S(1)}, u32[]{:S(2)}, u32[]{:S(2)}) collective-permute-start(bf16[24,4096]{1,0:T(8,128)(2,1)S(1)} %get-tuple-element.51), channel_id=1, source_target_pairs={{0,7},{1,6},{2,5},{3,4},{4,3},{5,2},{6,1},{7,0},{8,15},{9,14},{10,... | collective-permute-start | bytes 589832 | tf_op jit(solution)/shard_map/ppermute | solution.py:293
  136.5 0.1 collective-permute-done.12.refs_6_
  136.6 1.5 collective-permute-start.28
  138.1 3.7 %collective-permute-done.13.refs_7_ = bf16[24,4096]{1,0:T(8,128)(2,1)S(1)} collective-permute-done((bf16[24,4096]{1,0:T(8,128)(2,1)S(1)}, bf16[24,4096]{1,0:T(8,128)(2,1)S(1)}, u32[]{:S(2)}, u32[]{:S(2)}) %collective-permute-start.13) | collective-permute-done | bytes 196640 | tf_op jit(solution)/shard_map/ppermute | solution.py:293
  141.8 0.0 collective-permute-start.22
  141.8 0.0 collective-permute-done.27.refs_9_
  141.8 0.5 collective-permute-start.21
  142.3 0.0 collective-permute-done.24.refs_5_
  142.3 0.1 collective-permute-start.26
  142.3 0.0 collective-permute-done.23.refs_4_
  142.3 0.4 collective-permute-start.25
  142.8 1.6 collective-permute-done.28.refs_10_
  144.3 2.3 %combine.1 = bf16[128,4096]{1,0:T(8,128)(2,1)} custom-call(bf16[192,128]{1,0:T(8,128)(2,1)S(1)} %copy-done.3, bf16[24,4096]{1,0:T(8,128)(2,1)S(1)} %get-tuple-element.44.refs_0_, bf16[24,4096]{1,0:T(8,128)(2,1)S(1)} %collective-permute-done.7.refs_1_, bf16[24,4096]{1,0:T(8,128)(2,1)S(1)} %collective-permute-done.8.refs_2_, ...), custom_call_target="tpu_custom_call" | custom-call | flops 201326592 | bytes 2621440 | tf_op jit(solution)/shard_map/combine/pallas_call | solution.py:208
  146.7 9.0 %collective-permute-done.29.refs_11_ = bf16[192,1024]{1,0:T(8,128)(2,1)S(1)} collective-permute-done((bf16[192,1024]{1,0:T(8,128)(2,1)S(1)}, bf16[192,1024]{1,0:T(8,128)(2,1)S(1)}, u32[]{:S(2)}, u32[]{:S(2)}) %collective-permute-start.29) | collective-permute-done | bytes 393248 | tf_op jit(solution)/shard_map/ppermute | solution.py:293
  155.7 0.0 collective-permute-done.22.refs_3_
  155.7 10.0 %weight_grad.1 = bf16[4096,1024]{1,0:T(8,128)(2,1)} custom-call(bf16[96,4096]{1,0:T(8,128)(2,1)S(1)} %join_rows.2.refs_0_, bf16[96,4096]{1,0:T(8,128)(2,1)S(1)} %join_rows.3.refs_1_, bf16[96,4096]{1,0:T(8,128)(2,1)S(1)} %collective-permute-done.21.refs_2_, bf16[96,4096]{1,0:T(8,128)(2,1)S(1)} %collective-permute-done.22.refs_3_, ...), custom_call_target="tpu_custom_call" | custom-call | flops 6442450944 | bytes 16252928 | tf_op jit(solution)/shard_map/weight_grad/pallas_call | solution.py:275
  (12 shorter events, 0.0 us)
Async XLA Ops:
  4.7 11.4 %collective-permute-start = (bf16[24,4096]{1,0:T(8,128)(2,1)}, bf16[24,4096]{1,0:T(8,128)(2,1)S(1)}, u32[]{:S(2)}, u32[]{:S(2)}) collective-permute-start(bf16[24,4096]{1,0:T(8,128)(2,1)} %get-tuple-element.33), channel_id=1, source_target_pairs={{0,1},{1,0},{2,3},{3,2},{4,5},{5,4},{6,7},{7,6},{8,9},{9,8},{10,11... | collective-permute-start | bytes 589832 | tf_op jit(solution)/shard_map/ppermute | solution.py:293
  7.7 11.0 %collective-permute-start.1 = (bf16[24,4096]{1,0:T(8,128)(2,1)}, bf16[24,4096]{1,0:T(8,128)(2,1)S(1)}, u32[]{:S(2)}, u32[]{:S(2)}) collective-permute-start(bf16[24,4096]{1,0:T(8,128)(2,1)} %get-tuple-element.34), channel_id=1, source_target_pairs={{0,2},{1,3},{2,0},{3,1},{4,6},{5,7},{6,4},{7,5},{8,10},{9,11},{10,... | collective-permute-start | bytes 589832 | tf_op jit(solution)/shard_map/ppermute | solution.py:293
  9.3 1.2 copy-start
  10.5 0.8 copy-start.2
  12.6 6.5 %collective-permute-start.14 = (bf16[24,4096]{1,0:T(8,128)(2,1)S(1)}, bf16[24,4096]{1,0:T(8,128)(2,1)S(1)}, u32[]{:S(2)}, u32[]{:S(2)}) collective-permute-start(bf16[24,4096]{1,0:T(8,128)(2,1)S(1)} %get-tuple-element.53), channel_id=1, source_target_pairs={{0,1},{1,0},{2,3},{3,2},{4,5},{5,4},{6,7},{7,6},{8,9},{9,8},{10,11... | collective-permute-start | bytes 589832 | tf_op jit(solution)/shard_map/ppermute | solution.py:293
  13.2 14.3 %collective-permute-start.15 = (bf16[24,4096]{1,0:T(8,128)(2,1)S(1)}, bf16[24,4096]{1,0:T(8,128)(2,1)S(1)}, u32[]{:S(2)}, u32[]{:S(2)}) collective-permute-start(bf16[24,4096]{1,0:T(8,128)(2,1)S(1)} %get-tuple-element.54), channel_id=1, source_target_pairs={{0,2},{1,3},{2,0},{3,1},{4,6},{5,7},{6,4},{7,5},{8,10},{9,11},{10,... | collective-permute-start | bytes 589832 | tf_op jit(solution)/shard_map/ppermute | solution.py:293
  13.2 18.3 %collective-permute-start.16 = (bf16[24,4096]{1,0:T(8,128)(2,1)S(1)}, bf16[24,4096]{1,0:T(8,128)(2,1)S(1)}, u32[]{:S(2)}, u32[]{:S(2)}) collective-permute-start(bf16[24,4096]{1,0:T(8,128)(2,1)S(1)} %get-tuple-element.55), channel_id=1, source_target_pairs={{0,3},{1,2},{2,1},{3,0},{4,7},{5,6},{6,5},{7,4},{8,11},{9,10},{10,... | collective-permute-start | bytes 589832 | tf_op jit(solution)/shard_map/ppermute | solution.py:293
  16.1 15.4 %collective-permute-start.17 = (bf16[24,4096]{1,0:T(8,128)(2,1)S(1)}, bf16[24,4096]{1,0:T(8,128)(2,1)S(1)}, u32[]{:S(2)}, u32[]{:S(2)}) collective-permute-start(bf16[24,4096]{1,0:T(8,128)(2,1)S(1)} %get-tuple-element.56), channel_id=1, source_target_pairs={{0,4},{1,5},{2,6},{3,7},{4,0},{5,1},{6,2},{7,3},{8,12},{9,13},{10,... | collective-permute-start | bytes 589832 | tf_op jit(solution)/shard_map/ppermute | solution.py:293
  18.7 26.5 %collective-permute-start.18 = (bf16[24,4096]{1,0:T(8,128)(2,1)S(1)}, bf16[24,4096]{1,0:T(8,128)(2,1)S(1)}, u32[]{:S(2)}, u32[]{:S(2)}) collective-permute-start(bf16[24,4096]{1,0:T(8,128)(2,1)S(1)} %get-tuple-element.57), channel_id=1, source_target_pairs={{0,5},{1,4},{2,7},{3,6},{4,1},{5,0},{6,3},{7,2},{8,13},{9,12},{10,... | collective-permute-start | bytes 589832 | tf_op jit(solution)/shard_map/ppermute | solution.py:293
  19.0 26.2 %collective-permute-start.19 = (bf16[24,4096]{1,0:T(8,128)(2,1)S(1)}, bf16[24,4096]{1,0:T(8,128)(2,1)S(1)}, u32[]{:S(2)}, u32[]{:S(2)}) collective-permute-start(bf16[24,4096]{1,0:T(8,128)(2,1)S(1)} %get-tuple-element.58), channel_id=1, source_target_pairs={{0,6},{1,7},{2,4},{3,5},{4,2},{5,3},{6,0},{7,1},{8,14},{9,15},{10,... | collective-permute-start | bytes 589832 | tf_op jit(solution)/shard_map/ppermute | solution.py:293
  27.5 33.5 %collective-permute-start.20 = (bf16[24,4096]{1,0:T(8,128)(2,1)S(1)}, bf16[24,4096]{1,0:T(8,128)(2,1)S(1)}, u32[]{:S(2)}, u32[]{:S(2)}) collective-permute-start(bf16[24,4096]{1,0:T(8,128)(2,1)S(1)} %get-tuple-element.59), channel_id=1, source_target_pairs={{0,7},{1,6},{2,5},{3,4},{4,3},{5,2},{6,1},{7,0},{8,15},{9,14},{10,... | collective-permute-start | bytes 589832 | tf_op jit(solution)/shard_map/ppermute | solution.py:293
  31.5 30.6 %collective-permute-start.2 = (bf16[24,4096]{1,0:T(8,128)(2,1)}, bf16[24,4096]{1,0:T(8,128)(2,1)S(1)}, u32[]{:S(2)}, u32[]{:S(2)}) collective-permute-start(bf16[24,4096]{1,0:T(8,128)(2,1)} %get-tuple-element.35), channel_id=1, source_target_pairs={{0,3},{1,2},{2,1},{3,0},{4,7},{5,6},{6,5},{7,4},{8,11},{9,10},{10,... | collective-permute-start | bytes 589832 | tf_op jit(solution)/shard_map/ppermute | solution.py:293
  31.5 43.9 %collective-permute-start.3 = (bf16[24,4096]{1,0:T(8,128)(2,1)}, bf16[24,4096]{1,0:T(8,128)(2,1)S(1)}, u32[]{:S(2)}, u32[]{:S(2)}) collective-permute-start(bf16[24,4096]{1,0:T(8,128)(2,1)} %get-tuple-element.36), channel_id=1, source_target_pairs={{0,4},{1,5},{2,6},{3,7},{4,0},{5,1},{6,2},{7,3},{8,12},{9,13},{10,... | collective-permute-start | bytes 589832 | tf_op jit(solution)/shard_map/ppermute | solution.py:293
  45.2 33.7 %collective-permute-start.4 = (bf16[24,4096]{1,0:T(8,128)(2,1)}, bf16[24,4096]{1,0:T(8,128)(2,1)S(1)}, u32[]{:S(2)}, u32[]{:S(2)}) collective-permute-start(bf16[24,4096]{1,0:T(8,128)(2,1)} %get-tuple-element.37), channel_id=1, source_target_pairs={{0,5},{1,4},{2,7},{3,6},{4,1},{5,0},{6,3},{7,2},{8,13},{9,12},{10,... | collective-permute-start | bytes 589832 | tf_op jit(solution)/shard_map/ppermute | solution.py:293
  45.2 33.7 %collective-permute-start.5 = (bf16[24,4096]{1,0:T(8,128)(2,1)}, bf16[24,4096]{1,0:T(8,128)(2,1)S(1)}, u32[]{:S(2)}, u32[]{:S(2)}) collective-permute-start(bf16[24,4096]{1,0:T(8,128)(2,1)} %get-tuple-element.38), channel_id=1, source_target_pairs={{0,6},{1,7},{2,4},{3,5},{4,2},{5,3},{6,0},{7,1},{8,14},{9,15},{10,... | collective-permute-start | bytes 589832 | tf_op jit(solution)/shard_map/ppermute | solution.py:293
  61.0 17.9 %collective-permute-start.6 = (bf16[24,4096]{1,0:T(8,128)(2,1)}, bf16[24,4096]{1,0:T(8,128)(2,1)S(1)}, u32[]{:S(2)}, u32[]{:S(2)}) collective-permute-start(bf16[24,4096]{1,0:T(8,128)(2,1)} %get-tuple-element.39), channel_id=1, source_target_pairs={{0,7},{1,6},{2,5},{3,4},{4,3},{5,2},{6,1},{7,0},{8,15},{9,14},{10,... | collective-permute-start | bytes 589832 | tf_op jit(solution)/shard_map/ppermute | solution.py:293
  62.1 80.1 %collective-permute-start.24 = (bf16[96,4096]{1,0:T(8,128)(2,1)S(1)}, bf16[96,4096]{1,0:T(8,128)(2,1)S(1)}, u32[]{:S(2)}, u32[]{:S(2)}) collective-permute-start(bf16[96,4096]{1,0:T(8,128)(2,1)S(1)} %join_rows.3.refs_1_), channel_id=1, source_target_pairs={{0,16},{8,24},{16,0},{24,8},{1,17},{9,25},{17,1},{25,9},{2,18},{10... | collective-permute-start | bytes 2359304 | tf_op jit(solution)/shard_map/ppermute | solution.py:293
  75.4 66.9 %collective-permute-start.23 = (bf16[96,4096]{1,0:T(8,128)(2,1)S(1)}, bf16[96,4096]{1,0:T(8,128)(2,1)S(1)}, u32[]{:S(2)}, u32[]{:S(2)}) collective-permute-start(bf16[96,4096]{1,0:T(8,128)(2,1)S(1)} %join_rows.2.refs_0_), channel_id=1, source_target_pairs={{0,16},{8,24},{16,0},{24,8},{1,17},{9,25},{17,1},{25,9},{2,18},{10... | collective-permute-start | bytes 2359304 | tf_op jit(solution)/shard_map/ppermute | solution.py:293
  78.9 0.9 copy-start.1
  79.9 64.4 %copy-start.3 = (bf16[192,128]{1,0:T(8,128)(2,1)S(1)}, bf16[192,128]{1,0:T(8,128)(2,1)}, u32[]{:S(2)}) copy-start(bf16[192,128]{1,0:T(8,128)(2,1)} %get-tuple-element.31.one_hot_ref) | copy-start | bytes 147460
  97.2 9.1 %collective-permute-start.7 = (bf16[24,4096]{1,0:T(8,128)(2,1)S(1)}, bf16[24,4096]{1,0:T(8,128)(2,1)S(1)}, u32[]{:S(2)}, u32[]{:S(2)}) collective-permute-start(bf16[24,4096]{1,0:T(8,128)(2,1)S(1)} %get-tuple-element.45), channel_id=1, source_target_pairs={{0,1},{1,0},{2,3},{3,2},{4,5},{5,4},{6,7},{7,6},{8,9},{9,8},{10,11... | collective-permute-start | bytes 589832 | tf_op jit(solution)/shard_map/ppermute | solution.py:293
  99.5 15.8 %collective-permute-start.8 = (bf16[24,4096]{1,0:T(8,128)(2,1)S(1)}, bf16[24,4096]{1,0:T(8,128)(2,1)S(1)}, u32[]{:S(2)}, u32[]{:S(2)}) collective-permute-start(bf16[24,4096]{1,0:T(8,128)(2,1)S(1)} %get-tuple-element.46), channel_id=1, source_target_pairs={{0,2},{1,3},{2,0},{3,1},{4,6},{5,7},{6,4},{7,5},{8,10},{9,11},{10,... | collective-permute-start | bytes 589832 | tf_op jit(solution)/shard_map/ppermute | solution.py:293
  106.1 13.3 %collective-permute-start.9 = (bf16[24,4096]{1,0:T(8,128)(2,1)S(1)}, bf16[24,4096]{1,0:T(8,128)(2,1)S(1)}, u32[]{:S(2)}, u32[]{:S(2)}) collective-permute-start(bf16[24,4096]{1,0:T(8,128)(2,1)S(1)} %get-tuple-element.47), channel_id=1, source_target_pairs={{0,3},{1,2},{2,1},{3,0},{4,7},{5,6},{6,5},{7,4},{8,11},{9,10},{10,... | collective-permute-start | bytes 589832 | tf_op jit(solution)/shard_map/ppermute | solution.py:293
  106.3 22.6 %collective-permute-start.10 = (bf16[24,4096]{1,0:T(8,128)(2,1)S(1)}, bf16[24,4096]{1,0:T(8,128)(2,1)S(1)}, u32[]{:S(2)}, u32[]{:S(2)}) collective-permute-start(bf16[24,4096]{1,0:T(8,128)(2,1)S(1)} %get-tuple-element.48), channel_id=1, source_target_pairs={{0,4},{1,5},{2,6},{3,7},{4,0},{5,1},{6,2},{7,3},{8,12},{9,13},{10,... | collective-permute-start | bytes 589832 | tf_op jit(solution)/shard_map/ppermute | solution.py:293
  115.3 18.0 %collective-permute-start.11 = (bf16[24,4096]{1,0:T(8,128)(2,1)S(1)}, bf16[24,4096]{1,0:T(8,128)(2,1)S(1)}, u32[]{:S(2)}, u32[]{:S(2)}) collective-permute-start(bf16[24,4096]{1,0:T(8,128)(2,1)S(1)} %get-tuple-element.49), channel_id=1, source_target_pairs={{0,5},{1,4},{2,7},{3,6},{4,1},{5,0},{6,3},{7,2},{8,13},{9,12},{10,... | collective-permute-start | bytes 589832 | tf_op jit(solution)/shard_map/ppermute | solution.py:293
  119.4 22.3 %collective-permute-start.27 = (bf16[192,1024]{1,0:T(8,128)(2,1)S(1)}, bf16[192,1024]{1,0:T(8,128)(2,1)S(1)}, u32[]{:S(2)}, u32[]{:S(2)}) collective-permute-start(bf16[192,1024]{1,0:T(8,128)(2,1)S(1)} %get-tuple-element.41.refs_1_), channel_id=1, source_target_pairs={{0,8},{8,0},{16,24},{24,16},{1,9},{9,1},{17,25},{25,17},{2,10},{10... | collective-permute-start | bytes 1179656 | tf_op jit(solution)/shard_map/ppermute | solution.py:293
  129.0 7.6 %collective-permute-start.12 = (bf16[24,4096]{1,0:T(8,128)(2,1)S(1)}, bf16[24,4096]{1,0:T(8,128)(2,1)S(1)}, u32[]{:S(2)}, u32[]{:S(2)}) collective-permute-start(bf16[24,4096]{1,0:T(8,128)(2,1)S(1)} %get-tuple-element.50), channel_id=1, source_target_pairs={{0,6},{1,7},{2,4},{3,5},{4,2},{5,3},{6,0},{7,1},{8,14},{9,15},{10,... | collective-permute-start | bytes 589832 | tf_op jit(solution)/shard_map/ppermute | solution.py:293
  133.3 8.5 %collective-permute-start.13 = (bf16[24,4096]{1,0:T(8,128)(2,1)S(1)}, bf16[24,4096]{1,0:T(8,128)(2,1)S(1)}, u32[]{:S(2)}, u32[]{:S(2)}) collective-permute-start(bf16[24,4096]{1,0:T(8,128)(2,1)S(1)} %get-tuple-element.51), channel_id=1, source_target_pairs={{0,7},{1,6},{2,5},{3,4},{4,3},{5,2},{6,1},{7,0},{8,15},{9,14},{10,... | collective-permute-start | bytes 589832 | tf_op jit(solution)/shard_map/ppermute | solution.py:293
  136.6 7.8 %collective-permute-start.28 = (bf16[192,1024]{1,0:T(8,128)(2,1)S(1)}, bf16[192,1024]{1,0:T(8,128)(2,1)S(1)}, u32[]{:S(2)}, u32[]{:S(2)}) collective-permute-start(bf16[192,1024]{1,0:T(8,128)(2,1)S(1)} %get-tuple-element.42.refs_2_), channel_id=1, source_target_pairs={{0,16},{8,24},{16,0},{24,8},{1,17},{9,25},{17,1},{25,9},{2,18},{10... | collective-permute-start | bytes 1179656 | tf_op jit(solution)/shard_map/ppermute | solution.py:293
  141.8 13.9 %collective-permute-start.22 = (bf16[96,4096]{1,0:T(8,128)(2,1)S(1)}, bf16[96,4096]{1,0:T(8,128)(2,1)S(1)}, u32[]{:S(2)}, u32[]{:S(2)}) collective-permute-start(bf16[96,4096]{1,0:T(8,128)(2,1)S(1)} %join_rows.3.refs_1_), channel_id=1, source_target_pairs={{0,8},{8,0},{16,24},{24,16},{1,9},{9,1},{17,25},{25,17},{2,10},{10... | collective-permute-start | bytes 2359304 | tf_op jit(solution)/shard_map/ppermute | solution.py:293
  141.8 13.9 %collective-permute-start.21 = (bf16[96,4096]{1,0:T(8,128)(2,1)S(1)}, bf16[96,4096]{1,0:T(8,128)(2,1)S(1)}, u32[]{:S(2)}, u32[]{:S(2)}) collective-permute-start(bf16[96,4096]{1,0:T(8,128)(2,1)S(1)} %join_rows.2.refs_0_), channel_id=1, source_target_pairs={{0,8},{8,0},{16,24},{24,16},{1,9},{9,1},{17,25},{25,17},{2,10},{10... | collective-permute-start | bytes 2359304 | tf_op jit(solution)/shard_map/ppermute | solution.py:293
  142.3 13.4 %collective-permute-start.26 = (bf16[96,4096]{1,0:T(8,128)(2,1)S(1)}, bf16[96,4096]{1,0:T(8,128)(2,1)S(1)}, u32[]{:S(2)}, u32[]{:S(2)}) collective-permute-start(bf16[96,4096]{1,0:T(8,128)(2,1)S(1)} %collective-permute-done.24.refs_5_), channel_id=1, source_target_pairs={{0,8},{8,0},{16,24},{24,16},{1,9},{9,1},{17,25},{25,17},{2,10},{10... | collective-permute-start | bytes 2359304 | tf_op jit(solution)/shard_map/ppermute | solution.py:293
  142.3 13.3 %collective-permute-start.25 = (bf16[96,4096]{1,0:T(8,128)(2,1)S(1)}, bf16[96,4096]{1,0:T(8,128)(2,1)S(1)}, u32[]{:S(2)}, u32[]{:S(2)}) collective-permute-start(bf16[96,4096]{1,0:T(8,128)(2,1)S(1)} %collective-permute-done.23.refs_4_), channel_id=1, source_target_pairs={{0,8},{8,0},{16,24},{24,16},{1,9},{9,1},{17,25},{25,17},{2,10},{10... | collective-permute-start | bytes 2359304 | tf_op jit(solution)/shard_map/ppermute | solution.py:293
  144.3 11.3 %collective-permute-start.29 = (bf16[192,1024]{1,0:T(8,128)(2,1)S(1)}, bf16[192,1024]{1,0:T(8,128)(2,1)S(1)}, u32[]{:S(2)}, u32[]{:S(2)}) collective-permute-start(bf16[192,1024]{1,0:T(8,128)(2,1)S(1)} %get-tuple-element.43.refs_3_), channel_id=1, source_target_pairs={{0,24},{8,16},{16,8},{24,0},{1,25},{9,17},{17,9},{25,1},{2,26},{10... | collective-permute-start | bytes 1179656 | tf_op jit(solution)/shard_map/ppermute | solution.py:293
